TPU v7x, 32 devices: a whole 2x2x4 slice. The times are simulated.
32 devices in a mesh: section: 2 (over x), ctx: 16 (over z, y, core).
Axes of the slice: x: 2, y: 2, z: 4, core: 2. Of those that a mesh axis runs over, the one named last changes fastest.
Arguments:
- x_in: bfloat16 [512, 1536], P('ctx'), may hold values from -6 to 6
- stale_inputs: bfloat16 [2, 512, 1536], P('section', 'ctx'), may hold values from -6 to 6
- w_query: bfloat16 [2, 12, 128, 128], P('section'), may hold values from -0.5 to 0.5
- w_key: bfloat16 [2, 12, 128, 128], P('section'), may hold values from -0.5 to 0.5
- w_value: bfloat16 [2, 12, 128, 128], P('section'), may hold values from -0.5 to 0.5
- w_out: bfloat16 [2, 12, 128, 128], P('section'), may hold values from -0.5 to 0.5
- score_scale: float32 [2, 12], P('section'), may hold values from 1 to 3
- assign: int32 [512], P('ctx'), may hold values from 0 to 3, as said below
Outputs:
- section_out: bfloat16 [2, 512, 1536], P('section', 'ctx')
Inputs may be any that keep to these rules, and one draw needn't show every extreme that they name: `assign`: each aligned block of 32 tokens holds the same number of tokens of every micro-batch.
All inputs are finite; a program needn't handle non-finite values.
Results may differ from a plain program's by a relative error of at most 0.013.
Values may be sent and summed in bfloat16 or wider, within the bound.
No kernel may reach another device: no remote copies, remote signals or barrier semaphores. Data moves between devices by JAX's collectives and lax.ppermute only.
A program may use at most 128 MiB of HBM per device.

v0:
```python
import math
import jax
import jax.numpy as jnp
from jax import lax
from jax.sharding import PartitionSpec as P

MB = 4


def from_behind(array, axis, by):
    length = lax.axis_size(axis)
    pairs = [(i, i + by) for i in range(length) if 0 <= i + by < length]
    return lax.ppermute(array, axis, pairs)


def normalize(values):
    floats = values.astype(jnp.float32)
    return floats * lax.rsqrt(jnp.mean(floats * floats, axis=-1, keepdims=True) + 1e-06)


def project(normed, weight):
    count = normed.shape[0]
    return jnp.einsum(
        "nhd,hde->nhe",
        normed.reshape(count, weight.shape[0], weight.shape[1]),
        weight,
        preferred_element_type=jnp.float32,
    )


def key_pair(normed, w_key, w_value):
    count = normed.shape[0]
    keys = normalize(project(normed, w_key)).astype(jnp.bfloat16).reshape(count, -1)
    values = project(normed, w_value).astype(jnp.bfloat16).reshape(count, -1)
    return jnp.stack([keys, values])


def body(x_in, stale_inputs, w_query, w_key, w_value, w_out, score_scale, assign):
    tile_rows = x_in.shape[0]
    feature_width = x_in.shape[1]
    heads = w_query.shape[1]
    head_size = w_query.shape[2]
    query_weight = w_query[0]
    key_weight = w_key[0]
    value_weight = w_value[0]
    mix_weight = w_out[0]
    scales = score_scale[0]
    sections = lax.axis_size("section")
    section_index = lax.axis_index("section")
    ctx_index = lax.axis_index("ctx")
    per_batch = tile_rows // MB
    stale_normed = normalize(stale_inputs[0]).astype(jnp.bfloat16)
    pairs = lax.all_gather(
        key_pair(stale_normed, key_weight, value_weight), "ctx", axis=1, tiled=True
    )
    total = pairs.shape[1]
    far_keys = pairs[0].reshape(total, heads, head_size)
    far_values = pairs[1].reshape(total, heads, head_size)
    own_pair = lax.dynamic_slice_in_dim(pairs, ctx_index * tile_rows, tile_rows, 1)
    own_keys = own_pair[0].reshape(tile_rows, heads, head_size)
    own_values = own_pair[1].reshape(tile_rows, heads, head_size)
    far_mask = (jnp.arange(total, dtype=jnp.int32) // tile_rows != ctx_index).astype(jnp.float32)
    order = jnp.argsort(assign, stable=True)

    def advance(entering, batch_index, fresh_keys, fresh_values, rows):
        normed = normalize(entering).astype(jnp.bfloat16)
        queries = (
            normalize(project(normed, query_weight))
            * (scales[None, :, None] / math.sqrt(head_size))
        ).astype(jnp.bfloat16)
        new_keys = normalize(project(normed, key_weight)).astype(jnp.bfloat16)
        new_values = project(normed, value_weight).astype(jnp.bfloat16)
        fresh_keys = fresh_keys.at[rows].set(new_keys)
        fresh_values = fresh_values.at[rows].set(new_values)
        chosen = (assign <= batch_index).astype(jnp.float32)
        e_far = (
            jnp.exp(
                jnp.einsum("qhd,khd->hqk", queries, far_keys, preferred_element_type=jnp.float32)
            )
            * far_mask[None, None, :]
        )
        e_new = (
            jnp.exp(
                jnp.einsum("qhd,khd->hqk", queries, fresh_keys, preferred_element_type=jnp.float32)
            )
            * chosen[None, None, :]
        )
        e_old = (
            jnp.exp(
                jnp.einsum("qhd,khd->hqk", queries, own_keys, preferred_element_type=jnp.float32)
            )
            * (1.0 - chosen)[None, None, :]
        )
        denom = jnp.sum(e_far, -1) + jnp.sum(e_new, -1) + jnp.sum(e_old, -1)
        numer = jnp.einsum(
            "hqk,khd->qhd",
            e_far.astype(jnp.bfloat16),
            far_values,
            preferred_element_type=jnp.float32,
        )
        numer = numer + jnp.einsum(
            "hqk,khd->qhd",
            e_new.astype(jnp.bfloat16),
            fresh_values,
            preferred_element_type=jnp.float32,
        )
        numer = numer + jnp.einsum(
            "hqk,khd->qhd",
            e_old.astype(jnp.bfloat16),
            own_values,
            preferred_element_type=jnp.float32,
        )
        attended = (
            (numer / jnp.transpose(denom)[:, :, None])
            .astype(jnp.bfloat16)
            .reshape(per_batch, feature_width)
        )
        mixed = project(attended, mix_weight).reshape(per_batch, feature_width)
        return (
            (entering.astype(jnp.float32) + mixed).astype(jnp.bfloat16),
            fresh_keys,
            fresh_values,
        )

    def advance_step(moment, carry):
        incoming, out_buffer, fresh_keys, fresh_values = carry
        batch_index = moment - section_index
        valid = jnp.logical_and(batch_index >= 0, batch_index < MB)
        clamped = jnp.clip(batch_index, 0, MB - 1)
        rows = lax.dynamic_slice_in_dim(order, clamped * per_batch, per_batch)
        entering = jnp.where(section_index == 0, x_in[rows], incoming)
        result, next_keys, next_values = lax.cond(
            valid,
            lambda inputs: advance(*inputs),
            lambda inputs: (jnp.zeros_like(inputs[0]), inputs[2], inputs[3]),
            (entering, clamped, fresh_keys, fresh_values, rows),
        )
        out_buffer = jnp.where(valid, out_buffer.at[rows].set(result), out_buffer)
        incoming = from_behind(result, "section", 1)
        return (incoming, out_buffer, next_keys, next_values)

    initial = (
        jnp.zeros((per_batch, feature_width), jnp.bfloat16),
        jnp.zeros_like(x_in),
        jnp.zeros((tile_rows, heads, head_size), jnp.bfloat16),
        jnp.zeros((tile_rows, heads, head_size), jnp.bfloat16),
    )
    final = lax.fori_loop(0, MB + sections - 1, advance_step, initial)
    return final[1][None]


def solution(mesh):
    return jax.shard_map(
        body,
        mesh=mesh,
        in_specs=(
            P("ctx", None),
            P("section", "ctx", None),
            P("section", None, None, None),
            P("section", None, None, None),
            P("section", None, None, None),
            P("section", None, None, None),
            P("section", None),
            P("ctx"),
        ),
        out_specs=P("section", "ctx", None),
        check_vma=False,
    )
```

profile of v0, /device:TPU:0, one launch (start us, length us, event | category | flops | bytes accessed | tf_op | source)
XLA Modules:
  0.0 189.2 jit_solution(18121709102004149396)
XLA Ops:
  8.5 1.3 multiply_reduce_fusion.2
  12.3 2.3 %sort.17 = (s32[32]{0:T(128)}, s32[32]{0:T(128)}) sort(s32[32]{0:T(128)} %param.19, s32[32]{0:T(128)S(1)} %iota.7), dimensions={0}, to_apply=%region_0.0 | sort | flops 160 | bytes 512 | tf_op jit(solution)/shard_map/jit(argsort)/sort | solution.py:63
  14.7 46.0 %all-gather.2.cloned.1.call-done = bf16[2,512,1536]{2,1,0:T(8,128)(2,1)} async-done(((bf16[2,32,1536]{2,1,0:T(8,128)(2,1)}), bf16[2,512,1536]{2,1,0:T(8,128)(2,1)}) %all-gather.2.cloned.1.call-update) | async-done | bytes 3145744 | tf_op jit(solution)/shard_map/all_gather | solution.py:53
  63.1 3.2 %fusion.40 = (bf16[1,512,1536]{2,1,0:T(8,128)(2,1)}, bf16[1,512,1536]{2,1,0:T(8,128)(2,1)S(1)}) fusion(bf16[2,512,1536]{2,1,0:T(8,128)(2,1)} %all-gather.2.cloned.1.call-done), kind=kLoop, calls=%fused_computation.81 | loop fusion | bytes 6291456 | tf_op jit(solution)/shard_map/slice | solution.py:58
  68.0 2.6 %copy.33 = bf16[1,512,1536]{1,2,0:T(8,128)(2,1)} copy(bf16[1,512,1536]{2,1,0:T(8,128)(2,1)} %get-tuple-element.635) | data formatting | bytes 3145728 | tf_op jit(solution)/shard_map/slice | solution.py:58
  70.6 1.9 %copy.35 = bf16[512,12,128]{2,0,1:T(8,128)(2,1)S(1)} copy(bf16[512,12,128]{0,2,1:T(8,128)(2,1)} %bitcast.83) | data formatting | bytes 3145728
  73.9 107.9 %while.21 = (s32[]{:T(128)}, bf16[8,1536]{1,0:T(8,128)(2,1)S(1)}, bf16[32,1536]{1,0:T(8,128)(2,1)S(1)}, bf16[32,12,128]{2,1,0:T(8,128)(2,1)}, bf16[32,12,128]{2,...) while((s32[]{:T(128)}, bf16[8,1536]{1,0:T(8,128)(2,1)S(1)}, ...), condition=%wide.region_15.16_spmd.clone, body=%wide.region_3.15_spmd.clone.sunk | while | flops 41582888 | bytes 7045026 | solution.py:148
  74.6 15.7 %conditional.3 = (bf16[8,1536]{1,0:T(8,128)(2,1)S(1)}, bf16[32,12,128]{2,1,0:T(8,128)(2,1)}, bf16[32,12,128]{2,1,0:T(8,128)(2,1)}) conditional(s32[]{:T(128)} %convert_element_type.143, (bf16[32,12,128]{2,1,0:T(8,128)(2,1)}, bf16[32,12,128]{2,1,0:T(8,128)(2,1)}) %tuple.66, (pred[]{:T(512)}, bf16[32,1536]{1,0:T(8,128)(2,1)S(1)}, ...), branch_computations={%region_4.4_spmd, %region_5.13_spmd} | conditional | flops 41430252 | bytes 6378669 | solution.py:132
  75.4 1.3 multiply_reduce_fusion
  76.8 1.9 scatter_fusion.1
  78.7 1.3 multiply_reduce_fusion.1
  86.0 1.9 scatter_fusion
  88.9 1.4 fusion.3
  93.9 15.7 %conditional.3 = (bf16[8,1536]{1,0:T(8,128)(2,1)S(1)}, bf16[32,12,128]{2,1,0:T(8,128)(2,1)}, bf16[32,12,128]{2,1,0:T(8,128)(2,1)}) conditional(s32[]{:T(128)} %convert_element_type.143, (bf16[32,12,128]{2,1,0:T(8,128)(2,1)}, bf16[32,12,128]{2,1,0:T(8,128)(2,1)}) %tuple.66, (pred[]{:T(512)}, bf16[32,1536]{1,0:T(8,128)(2,1)S(1)}, ...), branch_computations={%region_4.4_spmd, %region_5.13_spmd} | conditional | flops 41430252 | bytes 6378669 | solution.py:132
  94.6 1.3 multiply_reduce_fusion
  96.1 1.9 scatter_fusion.1
  105.2 1.9 %scatter_fusion = bf16[32,12,128]{2,1,0:T(8,128)(2,1)} fusion(bf16[32,12,128]{2,1,0:T(8,128)(2,1)} %get-tuple-element.430, s32[8]{0:T(128)S(1)} %compare_select_fusion, bf16[8,12,128]{2,1,0:T(8,128)(2,1)S(1)} %copy.25), kind=kCustom, calls=%fused_computation.1 | custom fusion | bytes 73760 | tf_op jit(solution)/shard_map/while/body/eval_jaxpr/cond/branch_1_fun/scatter | solution.py:74
  108.2 1.4 fusion.3
  109.6 4.2 %collective-permute-start = (bf16[8,1536]{1,0:T(8,128)(2,1)S(1)}, bf16[8,1536]{1,0:T(8,128)(2,1)S(1)}, u32[]{:S(2)}, u32[]{:S(2)}) collective-permute-start(bf16[8,1536]{1,0:T(8,128)(2,1)S(1)} %get-tuple-element.772), channel_id=1, source_target_pairs={{0,16},{1,17},{2,18},{3,19},{4,20},{5,21},{6,22},{7,23},{8,24},{9,... | collective-permute-start | bytes 73736 | tf_op jit(solution)/shard_map/while/body/eval_jaxpr/ppermute | solution.py:13
  116.0 15.7 %conditional.3 = (bf16[8,1536]{1,0:T(8,128)(2,1)S(1)}, bf16[32,12,128]{2,1,0:T(8,128)(2,1)}, bf16[32,12,128]{2,1,0:T(8,128)(2,1)}) conditional(s32[]{:T(128)} %convert_element_type.143, (bf16[32,12,128]{2,1,0:T(8,128)(2,1)}, bf16[32,12,128]{2,1,0:T(8,128)(2,1)}) %tuple.66, (pred[]{:T(512)}, bf16[32,1536]{1,0:T(8,128)(2,1)S(1)}, ...), branch_computations={%region_4.4_spmd, %region_5.13_spmd} | conditional | flops 41430252 | bytes 6378669 | solution.py:132
  116.8 1.3 multiply_reduce_fusion
  118.3 1.9 scatter_fusion.1
  127.4 1.9 scatter_fusion
  130.3 1.4 fusion.3
  131.7 4.2 %collective-permute-start = (bf16[8,1536]{1,0:T(8,128)(2,1)S(1)}, bf16[8,1536]{1,0:T(8,128)(2,1)S(1)}, u32[]{:S(2)}, u32[]{:S(2)}) collective-permute-start(bf16[8,1536]{1,0:T(8,128)(2,1)S(1)} %get-tuple-element.772), channel_id=1, source_target_pairs={{0,16},{1,17},{2,18},{3,19},{4,20},{5,21},{6,22},{7,23},{8,24},{9,... | collective-permute-start | bytes 73736 | tf_op jit(solution)/shard_map/while/body/eval_jaxpr/ppermute | solution.py:13
  138.2 15.7 %conditional.3 = (bf16[8,1536]{1,0:T(8,128)(2,1)S(1)}, bf16[32,12,128]{2,1,0:T(8,128)(2,1)}, bf16[32,12,128]{2,1,0:T(8,128)(2,1)}) conditional(s32[]{:T(128)} %convert_element_type.143, (bf16[32,12,128]{2,1,0:T(8,128)(2,1)}, bf16[32,12,128]{2,1,0:T(8,128)(2,1)}) %tuple.66, (pred[]{:T(512)}, bf16[32,1536]{1,0:T(8,128)(2,1)S(1)}, ...), branch_computations={%region_4.4_spmd, %region_5.13_spmd} | conditional | flops 41430252 | bytes 6378669 | solution.py:132
  139.0 1.3 multiply_reduce_fusion
  140.4 1.9 scatter_fusion.1
  149.6 1.9 %scatter_fusion = bf16[32,12,128]{2,1,0:T(8,128)(2,1)} fusion(bf16[32,12,128]{2,1,0:T(8,128)(2,1)} %get-tuple-element.430, s32[8]{0:T(128)S(1)} %compare_select_fusion, bf16[8,12,128]{2,1,0:T(8,128)(2,1)S(1)} %copy.25), kind=kCustom, calls=%fused_computation.1 | custom fusion | bytes 73760 | tf_op jit(solution)/shard_map/while/body/eval_jaxpr/cond/branch_1_fun/scatter | solution.py:74
  152.5 1.4 fusion.3
  153.9 4.2 %collective-permute-start = (bf16[8,1536]{1,0:T(8,128)(2,1)S(1)}, bf16[8,1536]{1,0:T(8,128)(2,1)S(1)}, u32[]{:S(2)}, u32[]{:S(2)}) collective-permute-start(bf16[8,1536]{1,0:T(8,128)(2,1)S(1)} %get-tuple-element.772), channel_id=1, source_target_pairs={{0,16},{1,17},{2,18},{3,19},{4,20},{5,21},{6,22},{7,23},{8,24},{9,... | collective-permute-start | bytes 73736 | tf_op jit(solution)/shard_map/while/body/eval_jaxpr/ppermute | solution.py:13
  160.4 19.9 %collective-permute-start = (bf16[8,1536]{1,0:T(8,128)(2,1)S(1)}, bf16[8,1536]{1,0:T(8,128)(2,1)S(1)}, u32[]{:S(2)}, u32[]{:S(2)}) collective-permute-start(bf16[8,1536]{1,0:T(8,128)(2,1)S(1)} %get-tuple-element.772), channel_id=1, source_target_pairs={{0,16},{1,17},{2,18},{3,19},{4,20},{5,21},{6,22},{7,23},{8,24},{9,... | collective-permute-start | bytes 73736 | tf_op jit(solution)/shard_map/while/body/eval_jaxpr/ppermute | solution.py:13
  (150 shorter events, 58.0 us)
Async XLA Ops:
  6.5 54.1 %all-gather.2.cloned.1.call-start = ((), (), s32[]{:S(2)}) async-start(), calls=%async_computation | async-start | bytes 3342336 | tf_op jit(solution)/shard_map/all_gather | solution.py:53
  70.6 3.3 %copy-start = (bf16[32,1536]{1,0:T(8,128)(2,1)S(1)}, bf16[32,1536]{1,0:T(8,128)(2,1)}, u32[]{:S(2)}) copy-start(bf16[32,1536]{1,0:T(8,128)(2,1)} %param.12) | copy-start | bytes 294916
  90.3 2.8 %collective-permute-start = (bf16[8,1536]{1,0:T(8,128)(2,1)S(1)}, bf16[8,1536]{1,0:T(8,128)(2,1)S(1)}, u32[]{:S(2)}, u32[]{:S(2)}) collective-permute-start(bf16[8,1536]{1,0:T(8,128)(2,1)S(1)} %get-tuple-element.772), channel_id=1, source_target_pairs={{0,16},{1,17},{2,18},{3,19},{4,20},{5,21},{6,22},{7,23},{8,24},{9,... | collective-permute-start | bytes 73736 | tf_op jit(solution)/shard_map/while/body/eval_jaxpr/ppermute | solution.py:13
  109.6 5.7 %collective-permute-start = (bf16[8,1536]{1,0:T(8,128)(2,1)S(1)}, bf16[8,1536]{1,0:T(8,128)(2,1)S(1)}, u32[]{:S(2)}, u32[]{:S(2)}) collective-permute-start(bf16[8,1536]{1,0:T(8,128)(2,1)S(1)} %get-tuple-element.772), channel_id=1, source_target_pairs={{0,16},{1,17},{2,18},{3,19},{4,20},{5,21},{6,22},{7,23},{8,24},{9,... | collective-permute-start | bytes 73736 | tf_op jit(solution)/shard_map/while/body/eval_jaxpr/ppermute | solution.py:13
  131.7 5.8 %collective-permute-start = (bf16[8,1536]{1,0:T(8,128)(2,1)S(1)}, bf16[8,1536]{1,0:T(8,128)(2,1)S(1)}, u32[]{:S(2)}, u32[]{:S(2)}) collective-permute-start(bf16[8,1536]{1,0:T(8,128)(2,1)S(1)} %get-tuple-element.772), channel_id=1, source_target_pairs={{0,16},{1,17},{2,18},{3,19},{4,20},{5,21},{6,22},{7,23},{8,24},{9,... | collective-permute-start | bytes 73736 | tf_op jit(solution)/shard_map/while/body/eval_jaxpr/ppermute | solution.py:13
  153.9 5.7 %collective-permute-start = (bf16[8,1536]{1,0:T(8,128)(2,1)S(1)}, bf16[8,1536]{1,0:T(8,128)(2,1)S(1)}, u32[]{:S(2)}, u32[]{:S(2)}) collective-permute-start(bf16[8,1536]{1,0:T(8,128)(2,1)S(1)} %get-tuple-element.772), channel_id=1, source_target_pairs={{0,16},{1,17},{2,18},{3,19},{4,20},{5,21},{6,22},{7,23},{8,24},{9,... | collective-permute-start | bytes 73736 | tf_op jit(solution)/shard_map/while/body/eval_jaxpr/ppermute | solution.py:13
  160.4 21.4 %collective-permute-start = (bf16[8,1536]{1,0:T(8,128)(2,1)S(1)}, bf16[8,1536]{1,0:T(8,128)(2,1)S(1)}, u32[]{:S(2)}, u32[]{:S(2)}) collective-permute-start(bf16[8,1536]{1,0:T(8,128)(2,1)S(1)} %get-tuple-element.772), channel_id=1, source_target_pairs={{0,16},{1,17},{2,18},{3,19},{4,20},{5,21},{6,22},{7,23},{8,24},{9,... | collective-permute-start | bytes 73736 | tf_op jit(solution)/shard_map/while/body/eval_jaxpr/ppermute | solution.py:13
  181.8 0.6 copy-start.1
Sparse Core Ops, SparseCore 0:
  12.4 48.1 all-gather.1
where the time goes:
time: 191 us; the launch traced here: 189 us
  waiting for transfers between devices  49.4 us (26%)
  matrix products  40.7 us (21%)
  local copies, waits for them, and re-layouts  36.2 us (19%)
  starting transfers between devices  33.8 us (18%)
  other arithmetic  15 us (8%)
  between operations  13.5 us (7%)
    all_gather x1, waiting for transfers between devices, body(): lax.all_gather(key_pair(stale_normed, key_weight, value_weight), 'ctx', a...  46 us
    ppermute x5, starting transfers between devices, from_behind(): return lax.ppermute(array, axis, pairs)  33.8 us
    dot_general x18, matrix products, project(): jnp.einsum('nhd,hde->nhe', normed.reshape(count, weight.shape[0], weight....  23.7 us
    scatter x4, local copies, waits for them, and re-layouts, advance(): fresh_values = fresh_values.at[rows].set(new_values)  7.57 us
    scatter x4, local copies, waits for them, and re-layouts, advance(): fresh_keys = fresh_keys.at[rows].set(new_keys)  7.53 us
    slice x2, local copies, waits for them, and re-layouts, body(): far_values = pairs[1].reshape(total, heads, head_size)  5.84 us
    unnamed x8, local copies, waits for them, and re-layouts  4.81 us
    dot_general x4, matrix products, advance(): jnp.einsum('qhd,khd->hqk', queries, fresh_keys, preferred_element_type=jn...  4.58 us
  transfers between devices with their start and end apart: 6, of which 6 were waited for; matrix products, arithmetic and copies ran while one was open for 3% of the time, Pallas kernels for 0%

commit v1 on v0

--- a/solution.py
+++ b/solution.py
@@ -5,6 +5,18 @@
 from jax.sharding import PartitionSpec as P
 
 MB = 4
+
+
+def gather_by_bits(array, axis, dim):
+    ways, here = (lax.axis_size(axis), lax.axis_index(axis))
+    grown, reach = (array, 1)
+    while reach < ways:
+        theirs = lax.ppermute(grown, axis, [(d, d ^ reach) for d in range(ways)])
+        mine_first = jnp.concatenate([grown, theirs], axis=dim)
+        theirs_first = jnp.concatenate([theirs, grown], axis=dim)
+        grown = jnp.where(here & reach == 0, mine_first, theirs_first)
+        reach = 2 * reach
+    return grown
 
 
 def from_behind(array, axis, by):
@@ -50,9 +62,7 @@
     ctx_index = lax.axis_index("ctx")
     per_batch = tile_rows // MB
     stale_normed = normalize(stale_inputs[0]).astype(jnp.bfloat16)
-    pairs = lax.all_gather(
-        key_pair(stale_normed, key_weight, value_weight), "ctx", axis=1, tiled=True
-    )
+    pairs = gather_by_bits(key_pair(stale_normed, key_weight, value_weight), "ctx", 1)
     total = pairs.shape[1]
     far_keys = pairs[0].reshape(total, heads, head_size)
     far_values = pairs[1].reshape(total, heads, head_size)

time: 191 us -> 254 us (1.33)
  waiting for transfers between devices: 49.4 us -> 93.1 us
  starting transfers between devices: 33.8 us -> 49.3 us
  between operations: 13.5 us -> 0.16 us
  other arithmetic: 15 us -> 26.1 us
  local copies, waits for them, and re-layouts: 36.2 us -> 39.4 us
    ppermute x0 -> x4, waiting for transfers between devices: none -> 92.6 us  [gather_by_bits(): theirs = lax.ppermute(grown, axis, [(d, d ^ reach) for d in range(ways)])]
    all_gather x1 -> x0, waiting for transfers between devices: 46 us -> none  [body(): lax.all_gather(key_pair(stale_normed, key_weight, value_weight), 'ctx', a...]
    ppermute x0 -> x4, starting transfers between devices: none -> 7.95 us  [gather_by_bits(): theirs = lax.ppermute(grown, axis, [(d, d ^ reach) for d in range(ways)])]
    ppermute x5, starting transfers between devices: 33.8 us -> 41.3 us  [from_behind(): return lax.ppermute(array, axis, pairs)]
    select_n x0 -> x4, other arithmetic: none -> 4.56 us  [gather_by_bits(): grown = jnp.where(here & reach == 0, mine_first, theirs_first)]
    select_n x5, other arithmetic: 3.69 us -> 6.64 us  [advance_step(): entering = jnp.where(section_index == 0, x_in[rows], incoming)]
    ppermute x5, waiting for transfers between devices: 3.39 us -> 0.52 us  [from_behind(): return lax.ppermute(array, axis, pairs)]
    unnamed x8 -> x13, local copies, waits for them, and re-layouts: 4.81 us -> 5.39 us
  transfers between devices with their start and end apart: 6 -> 9, of which waited for: 6 -> 9; matrix products, arithmetic and copies ran while one was open for 3% -> 3% of each run, Pallas kernels for 0% -> 0%
where the time goes in v1:
time: 254 us; the launch traced here: 252 us
  waiting for transfers between devices  93.1 us (37%)
  starting transfers between devices  49.3 us (19%)
  matrix products  43.2 us (17%)
  local copies, waits for them, and re-layouts  39.4 us (16%)
  other arithmetic  26.1 us (10%)
    ppermute x4, waiting for transfers between devices, gather_by_bits(): theirs = lax.ppermute(grown, axis, [(d, d ^ reach) for d in range(ways)])  92.6 us
    ppermute x5, starting transfers between devices, from_behind(): return lax.ppermute(array, axis, pairs)  41.3 us
    dot_general x18, matrix products, project(): jnp.einsum('nhd,hde->nhe', normed.reshape(count, weight.shape[0], weight....  26.2 us
    scatter x4, local copies, waits for them, and re-layouts, advance(): fresh_values = fresh_values.at[rows].set(new_values)  8.05 us
    ppermute x4, starting transfers between devices, gather_by_bits(): theirs = lax.ppermute(grown, axis, [(d, d ^ reach) for d in range(ways)])  7.95 us
    scatter x4, local copies, waits for them, and re-layouts, advance(): fresh_keys = fresh_keys.at[rows].set(new_keys)  7.56 us
    select_n x5, other arithmetic, advance_step(): entering = jnp.where(section_index == 0, x_in[rows], incoming)  6.64 us
    unnamed x13, local copies, waits for them, and re-layouts  5.39 us
  transfers between devices with their start and end apart: 9, of which 9 were waited for; matrix products, arithmetic and copies ran while one was open for 3% of the time, Pallas kernels for 0%

profile of v1, /device:TPU:0, one launch (start us, length us, event | category | flops | bytes accessed | tf_op | source)
XLA Modules:
  0.0 251.6 jit_solution(9674841952983971367)
XLA Ops:
  6.8 2.9 %collective-permute-start.2 = (bf16[2,64,1536]{2,1,0:T(8,128)(2,1)S(1)}, bf16[2,64,1536]{2,1,0:T(8,128)(2,1)S(1)}, u32[]{:S(2)}, u32[]{:S(2)}) collective-permute-start(bf16[2,64,1536]{2,1,0:T(8,128)(2,1)S(1)} %maximum_select_fusion.3), channel_id=1, source_target_pairs={{0,2},{1,3},{2,0},{3,1},{4,6},{5,7},{6,4},{7,5},{8,10},{9,11},{10,... | collective-permute-start | bytes 1179656 | tf_op jit(solution)/shard_map/ppermute | solution.py:14
  9.7 9.4 %collective-permute-done.2 = bf16[2,64,1536]{2,1,0:T(8,128)(2,1)S(1)} collective-permute-done((bf16[2,64,1536]{2,1,0:T(8,128)(2,1)S(1)}, bf16[2,64,1536]{2,1,0:T(8,128)(2,1)S(1)}, u32[]{:S(2)}, u32[]{:S(2)}) %collective-permute-start.2) | collective-permute-done | bytes 393248 | tf_op jit(solution)/shard_map/ppermute | solution.py:14
  21.2 17.2 %collective-permute-done.3 = bf16[2,128,1536]{2,1,0:T(8,128)(2,1)S(1)} collective-permute-done((bf16[2,128,1536]{2,1,0:T(8,128)(2,1)S(1)}, bf16[2,128,1536]{2,1,0:T(8,128)(2,1)S(1)}, u32[]{:S(2)}, u32[]{:S(2)}) %collective-permute-start.3) | collective-permute-done | bytes 786464 | tf_op jit(solution)/shard_map/ppermute | solution.py:14
  39.0 2.6 %collective-permute-start.4 = (bf16[2,256,1536]{2,1,0:T(8,128)(2,1)S(1)}, bf16[2,256,1536]{2,1,0:T(8,128)(2,1)}, u32[]{:S(2)}, u32[]{:S(2)}) collective-permute-start(bf16[2,256,1536]{2,1,0:T(8,128)(2,1)S(1)} %maximum_select_fusion.1), channel_id=1, source_target_pairs={{0,8},{1,9},{2,10},{3,11},{4,12},{5,13},{6,14},{7,15},{8,0},{9,1},... | collective-permute-start | bytes 4718600 | tf_op jit(solution)/shard_map/ppermute | solution.py:14
  41.6 2.3 sort.17
  43.9 64.9 %collective-permute-done.4 = bf16[2,256,1536]{2,1,0:T(8,128)(2,1)} collective-permute-done((bf16[2,256,1536]{2,1,0:T(8,128)(2,1)S(1)}, bf16[2,256,1536]{2,1,0:T(8,128)(2,1)}, u32[]{:S(2)}, u32[]{:S(2)}) %collective-permute-start.4) | collective-permute-done | bytes 1572896 | tf_op jit(solution)/shard_map/ppermute | solution.py:14
  108.8 3.7 %maximum_select_fusion = bf16[2,512,1536]{2,1,0:T(8,128)(2,1)S(1)} fusion(bf16[2,256,1536]{2,1,0:T(8,128)(2,1)} %collective-permute-done.4, bf16[2,256,1536]{2,1,0:T(8,128)(2,1)} %copy-done.3, pred[]{:T(512)S(6)} %eq.22), kind=kLoop, calls=%fused_computation.63 | loop fusion | flops 14155776 | bytes 6291457 | tf_op jit(solution)/shard_map/jit(_where)/select_n | solution.py:17
  112.5 2.1 fusion.40
  120.3 2.6 %copy.32 = bf16[1,512,1536]{1,2,0:T(8,128)(2,1)} copy(bf16[1,512,1536]{2,1,0:T(8,128)(2,1)} %get-tuple-element.636) | data formatting | bytes 3145728 | tf_op jit(solution)/shard_map/slice | solution.py:67
  122.9 1.9 copy.34
  126.8 124.2 %while.21 = (s32[]{:T(128)}, bf16[8,1536]{1,0:T(8,128)(2,1)}, bf16[32,1536]{1,0:T(8,128)(2,1)S(1)}, bf16[32,12,128]{2,1,0:T(8,128)(2,1)}, bf16[32,12,128]{2,1,0:...) while((s32[]{:T(128)}, bf16[8,1536]{1,0:T(8,128)(2,1)}, ...), condition=%wide.region_15.16_spmd.clone, body=%wide.region_3.15_spmd.clone.sunk | while | flops 41582888 | bytes 7045182 | solution.py:158
  128.1 17.5 %conditional.3 = (bf16[8,1536]{1,0:T(8,128)(2,1)}, bf16[32,12,128]{2,1,0:T(8,128)(2,1)}, bf16[32,12,128]{2,1,0:T(8,128)(2,1)}) conditional(s32[]{:T(128)} %convert_element_type.143, (bf16[32,12,128]{2,1,0:T(8,128)(2,1)}, bf16[32,12,128]{2,1,0:T(8,128)(2,1)}) %tuple.66, (pred[]{:T(512)}, bf16[32,1536]{1,0:T(8,128)(2,1)S(1)}, s32[8,1]{0,1:T(1,128)S(1)}, ...), branch_computations={%region_4.4_spmd, %region_5.13_spmd} | conditional | flops 41430252 | bytes 6378825 | solution.py:142
  137.5 1.9 scatter_fusion.1
  140.5 2.0 scatter_fusion
  143.6 2.0 fusion.3
  145.6 1.9 collective-permute-start
  149.9 17.5 %conditional.3 = (bf16[8,1536]{1,0:T(8,128)(2,1)}, bf16[32,12,128]{2,1,0:T(8,128)(2,1)}, bf16[32,12,128]{2,1,0:T(8,128)(2,1)}) conditional(s32[]{:T(128)} %convert_element_type.143, (bf16[32,12,128]{2,1,0:T(8,128)(2,1)}, bf16[32,12,128]{2,1,0:T(8,128)(2,1)}) %tuple.66, (pred[]{:T(512)}, bf16[32,1536]{1,0:T(8,128)(2,1)S(1)}, s32[8,1]{0,1:T(1,128)S(1)}, ...), branch_computations={%region_4.4_spmd, %region_5.13_spmd} | conditional | flops 41430252 | bytes 6378825 | solution.py:142
  159.3 1.9 scatter_fusion.1
  162.4 2.0 scatter_fusion
  165.4 2.0 fusion.3
  167.4 5.6 %collective-permute-start = (bf16[8,1536]{1,0:T(8,128)(2,1)}, bf16[8,1536]{1,0:T(8,128)(2,1)}, u32[]{:S(2)}, u32[]{:S(2)}) collective-permute-start(bf16[8,1536]{1,0:T(8,128)(2,1)} %get-tuple-element.772), channel_id=1, source_target_pairs={{0,16},{1,17},{2,18},{3,19},{4,20},{5,21},{6,22},{7,23},{8,24},{9,... | collective-permute-start | bytes 73736 | tf_op jit(solution)/shard_map/while/body/eval_jaxpr/ppermute | solution.py:25
  175.5 17.5 %conditional.3 = (bf16[8,1536]{1,0:T(8,128)(2,1)}, bf16[32,12,128]{2,1,0:T(8,128)(2,1)}, bf16[32,12,128]{2,1,0:T(8,128)(2,1)}) conditional(s32[]{:T(128)} %convert_element_type.143, (bf16[32,12,128]{2,1,0:T(8,128)(2,1)}, bf16[32,12,128]{2,1,0:T(8,128)(2,1)}) %tuple.66, (pred[]{:T(512)}, bf16[32,1536]{1,0:T(8,128)(2,1)S(1)}, s32[8,1]{0,1:T(1,128)S(1)}, ...), branch_computations={%region_4.4_spmd, %region_5.13_spmd} | conditional | flops 41430252 | bytes 6378825 | solution.py:142
  184.9 1.9 scatter_fusion.1
  187.9 2.0 scatter_fusion
  191.0 2.0 fusion.3
  193.0 5.7 %collective-permute-start = (bf16[8,1536]{1,0:T(8,128)(2,1)}, bf16[8,1536]{1,0:T(8,128)(2,1)}, u32[]{:S(2)}, u32[]{:S(2)}) collective-permute-start(bf16[8,1536]{1,0:T(8,128)(2,1)} %get-tuple-element.772), channel_id=1, source_target_pairs={{0,16},{1,17},{2,18},{3,19},{4,20},{5,21},{6,22},{7,23},{8,24},{9,... | collective-permute-start | bytes 73736 | tf_op jit(solution)/shard_map/while/body/eval_jaxpr/ppermute | solution.py:25
  201.1 17.5 %conditional.3 = (bf16[8,1536]{1,0:T(8,128)(2,1)}, bf16[32,12,128]{2,1,0:T(8,128)(2,1)}, bf16[32,12,128]{2,1,0:T(8,128)(2,1)}) conditional(s32[]{:T(128)} %convert_element_type.143, (bf16[32,12,128]{2,1,0:T(8,128)(2,1)}, bf16[32,12,128]{2,1,0:T(8,128)(2,1)}) %tuple.66, (pred[]{:T(512)}, bf16[32,1536]{1,0:T(8,128)(2,1)S(1)}, s32[8,1]{0,1:T(1,128)S(1)}, ...), branch_computations={%region_4.4_spmd, %region_5.13_spmd} | conditional | flops 41430252 | bytes 6378825 | solution.py:142
  210.5 1.9 scatter_fusion.1
  213.6 2.0 scatter_fusion
  216.6 2.0 fusion.3
  218.6 5.6 %collective-permute-start = (bf16[8,1536]{1,0:T(8,128)(2,1)}, bf16[8,1536]{1,0:T(8,128)(2,1)}, u32[]{:S(2)}, u32[]{:S(2)}) collective-permute-start(bf16[8,1536]{1,0:T(8,128)(2,1)} %get-tuple-element.772), channel_id=1, source_target_pairs={{0,16},{1,17},{2,18},{3,19},{4,20},{5,21},{6,22},{7,23},{8,24},{9,... | collective-permute-start | bytes 73736 | tf_op jit(solution)/shard_map/while/body/eval_jaxpr/ppermute | solution.py:25
  227.3 22.5 %collective-permute-start = (bf16[8,1536]{1,0:T(8,128)(2,1)}, bf16[8,1536]{1,0:T(8,128)(2,1)}, u32[]{:S(2)}, u32[]{:S(2)}) collective-permute-start(bf16[8,1536]{1,0:T(8,128)(2,1)} %get-tuple-element.772), channel_id=1, source_target_pairs={{0,16},{1,17},{2,18},{3,19},{4,20},{5,21},{6,22},{7,23},{8,24},{9,... | collective-permute-start | bytes 73736 | tf_op jit(solution)/shard_map/while/body/eval_jaxpr/ppermute | solution.py:25
  (172 shorter events, 77.0 us)
Async XLA Ops:
  5.1 1.6 collective-permute-start.1
  6.8 12.4 %collective-permute-start.2 = (bf16[2,64,1536]{2,1,0:T(8,128)(2,1)S(1)}, bf16[2,64,1536]{2,1,0:T(8,128)(2,1)S(1)}, u32[]{:S(2)}, u32[]{:S(2)}) collective-permute-start(bf16[2,64,1536]{2,1,0:T(8,128)(2,1)S(1)} %maximum_select_fusion.3), channel_id=1, source_target_pairs={{0,2},{1,3},{2,0},{3,1},{4,6},{5,7},{6,4},{7,5},{8,10},{9,11},{10,... | collective-permute-start | bytes 1179656 | tf_op jit(solution)/shard_map/ppermute | solution.py:14
  19.3 19.1 %collective-permute-start.3 = (bf16[2,128,1536]{2,1,0:T(8,128)(2,1)S(1)}, bf16[2,128,1536]{2,1,0:T(8,128)(2,1)S(1)}, u32[]{:S(2)}, u32[]{:S(2)}) collective-permute-start(bf16[2,128,1536]{2,1,0:T(8,128)(2,1)S(1)} %maximum_select_fusion.2), channel_id=1, source_target_pairs={{0,4},{1,5},{2,6},{3,7},{4,0},{5,1},{6,2},{7,3},{8,12},{9,13},{10,... | collective-permute-start | bytes 2359304 | tf_op jit(solution)/shard_map/ppermute | solution.py:14
  39.0 4.9 %copy-start.3 = (bf16[2,256,1536]{2,1,0:T(8,128)(2,1)}, bf16[2,256,1536]{2,1,0:T(8,128)(2,1)S(1)}, u32[]{:S(2)}) copy-start(bf16[2,256,1536]{2,1,0:T(8,128)(2,1)S(1)} %maximum_select_fusion.1) | copy-start | bytes 4718596
  39.0 69.8 %collective-permute-start.4 = (bf16[2,256,1536]{2,1,0:T(8,128)(2,1)S(1)}, bf16[2,256,1536]{2,1,0:T(8,128)(2,1)}, u32[]{:S(2)}, u32[]{:S(2)}) collective-permute-start(bf16[2,256,1536]{2,1,0:T(8,128)(2,1)S(1)} %maximum_select_fusion.1), channel_id=1, source_target_pairs={{0,8},{1,9},{2,10},{3,11},{4,12},{5,13},{6,14},{7,15},{8,0},{9,1},... | collective-permute-start | bytes 4718600 | tf_op jit(solution)/shard_map/ppermute | solution.py:14
  112.5 2.6 %copy-start = (bf16[2,512,1536]{2,1,0:T(8,128)(2,1)}, bf16[2,512,1536]{2,1,0:T(8,128)(2,1)S(1)}, u32[]{:S(2)}) copy-start(bf16[2,512,1536]{2,1,0:T(8,128)(2,1)S(1)} %maximum_select_fusion) | copy-start | bytes 9437188
  122.9 3.9 %copy-start.1 = (bf16[32,1536]{1,0:T(8,128)(2,1)S(1)}, bf16[32,1536]{1,0:T(8,128)(2,1)}, u32[]{:S(2)}) copy-start(bf16[32,1536]{1,0:T(8,128)(2,1)} %param.12) | copy-start | bytes 294916
  135.4 2.1 copy-start.4
  145.6 3.0 %collective-permute-start = (bf16[8,1536]{1,0:T(8,128)(2,1)}, bf16[8,1536]{1,0:T(8,128)(2,1)}, u32[]{:S(2)}, u32[]{:S(2)}) collective-permute-start(bf16[8,1536]{1,0:T(8,128)(2,1)} %get-tuple-element.772), channel_id=1, source_target_pairs={{0,16},{1,17},{2,18},{3,19},{4,20},{5,21},{6,22},{7,23},{8,24},{9,... | collective-permute-start | bytes 73736 | tf_op jit(solution)/shard_map/while/body/eval_jaxpr/ppermute | solution.py:25
  157.2 2.1 copy-start.4
  167.4 6.7 %collective-permute-start = (bf16[8,1536]{1,0:T(8,128)(2,1)}, bf16[8,1536]{1,0:T(8,128)(2,1)}, u32[]{:S(2)}, u32[]{:S(2)}) collective-permute-start(bf16[8,1536]{1,0:T(8,128)(2,1)} %get-tuple-element.772), channel_id=1, source_target_pairs={{0,16},{1,17},{2,18},{3,19},{4,20},{5,21},{6,22},{7,23},{8,24},{9,... | collective-permute-start | bytes 73736 | tf_op jit(solution)/shard_map/while/body/eval_jaxpr/ppermute | solution.py:25
  182.8 2.1 copy-start.4
  193.0 6.8 %collective-permute-start = (bf16[8,1536]{1,0:T(8,128)(2,1)}, bf16[8,1536]{1,0:T(8,128)(2,1)}, u32[]{:S(2)}, u32[]{:S(2)}) collective-permute-start(bf16[8,1536]{1,0:T(8,128)(2,1)} %get-tuple-element.772), channel_id=1, source_target_pairs={{0,16},{1,17},{2,18},{3,19},{4,20},{5,21},{6,22},{7,23},{8,24},{9,... | collective-permute-start | bytes 73736 | tf_op jit(solution)/shard_map/while/body/eval_jaxpr/ppermute | solution.py:25
  208.4 2.1 copy-start.4
  218.6 6.7 %collective-permute-start = (bf16[8,1536]{1,0:T(8,128)(2,1)}, bf16[8,1536]{1,0:T(8,128)(2,1)}, u32[]{:S(2)}, u32[]{:S(2)}) collective-permute-start(bf16[8,1536]{1,0:T(8,128)(2,1)} %get-tuple-element.772), channel_id=1, source_target_pairs={{0,16},{1,17},{2,18},{3,19},{4,20},{5,21},{6,22},{7,23},{8,24},{9,... | collective-permute-start | bytes 73736 | tf_op jit(solution)/shard_map/while/body/eval_jaxpr/ppermute | solution.py:25
  227.3 23.6 %collective-permute-start = (bf16[8,1536]{1,0:T(8,128)(2,1)}, bf16[8,1536]{1,0:T(8,128)(2,1)}, u32[]{:S(2)}, u32[]{:S(2)}) collective-permute-start(bf16[8,1536]{1,0:T(8,128)(2,1)} %get-tuple-element.772), channel_id=1, source_target_pairs={{0,16},{1,17},{2,18},{3,19},{4,20},{5,21},{6,22},{7,23},{8,24},{9,... | collective-permute-start | bytes 73736 | tf_op jit(solution)/shard_map/while/body/eval_jaxpr/ppermute | solution.py:25
  250.9 0.6 copy-start.2
